TPU v7x, 512 devices: a whole 4x8x8 slice. The times are simulated.
512 devices in a mesh: space: 32 (over y, z_hi), tensor: 16 (over x, z_lo, core).
Axes of the slice: x: 4, y: 8, z: 8 (z_hi: 4, z_lo: 2; z = z_hi * 2 + z_lo), core: 2. Of those that a mesh axis runs over, the one named last changes fastest.
Arguments:
- features: bfloat16 [128, 128, 1024], P('space', None, 'tensor'), may hold values from -6 to 6
- depth_kernel: bfloat16 [2, 7, 7, 1024], P(None, None, None, 'tensor'), may hold values from -5 to 5
- norm_gain: float32 [2, 1024], replicated, may hold values from 0.5 to 1.5
- norm_bias: float32 [2, 1024], replicated, may hold values from -3 to 3
- w_expand: bfloat16 [2, 1024, 4096], P(None, None, 'tensor'), may hold values from -0.1875 to 0.1875
- b_expand: float32 [2, 4096], P(None, 'tensor'), may hold values from -3 to 3
- w_reduce: bfloat16 [2, 4096, 1024], P(None, 'tensor'), may hold values from -0.125 to 0.125
- b_reduce: float32 [2, 1024], P(None, 'tensor'), may hold values from -3 to 3
- layer_scale: float32 [2, 1024], P(None, 'tensor'), may hold values from 0.5 to 1.5
Outputs:
- output: bfloat16 [128, 128, 1024], P('space', None, 'tensor')
All inputs are finite; a program needn't handle non-finite values.
Results may differ from a plain program's by a relative error of at most 0.023.
Values may be sent and summed in bfloat16 or wider, within the bound.
No kernel may reach another device: no remote copies, remote signals or barrier semaphores. Data moves between devices by JAX's collectives and lax.ppermute only.
A program may use at most 64 MiB of HBM per device.

v0:
```python
import jax
import jax.numpy as jnp
from jax import lax
from jax.sharding import PartitionSpec as P

D = 1024
TAPS = 7
BLOCKS = 2


def with_halo(x, sides, width):
    for axis, dim in sides:
        devices, length = (lax.axis_size(axis), x.shape[dim])
        up = [(i, (i + 1) % devices) for i in range(devices - 1)]
        down = [(j, i) for i, j in up]
        last = lax.slice_in_dim(x, length - width, length, axis=dim)
        leading = lax.slice_in_dim(x, 0, width, axis=dim)
        before = lax.ppermute(last, axis, up)
        after = lax.ppermute(leading, axis, down)
        x = jnp.concatenate([before, x, after], axis=dim)
    return x


def one_block(stream, kernel, gain, bias, expand, bias_expand, reduce_w, bias_reduce, scale):
    half = TAPS // 2
    height, width, share = stream.shape
    positions = height * width
    padded = with_halo(stream, (("space", 0),), half)
    padded = jnp.pad(padded.astype(jnp.float32), ((0, 0), (half, half), (0, 0)))
    filtered = jnp.zeros(stream.shape, jnp.float32)
    for row_tap in range(TAPS):
        for col_tap in range(TAPS):
            filtered = filtered + padded[
                row_tap : row_tap + height, col_tap : col_tap + width
            ] * kernel[row_tap, col_tap].astype(jnp.float32)
    filtered = filtered.reshape(positions, share)
    offset = lax.axis_index("tensor") * share
    gain_part = lax.dynamic_slice_in_dim(gain, offset, share, 0)
    bias_part = lax.dynamic_slice_in_dim(bias, offset, share, 0)
    sums, squares = lax.psum(
        (jnp.sum(filtered, axis=-1), jnp.sum(filtered * filtered, axis=-1)), "tensor"
    )
    mean = (sums / D)[:, None]
    var = jnp.maximum(squares[:, None] / D - mean * mean, 0.0)
    normed_part = ((filtered - mean) / jnp.sqrt(var + 1e-06) * gain_part + bias_part).astype(
        jnp.bfloat16
    )
    preact = jnp.dot(
        lax.all_gather(normed_part, "tensor", axis=1, tiled=True),
        expand,
        preferred_element_type=jnp.float32,
    )
    hidden = jax.nn.gelu(preact + bias_expand, approximate=False).astype(jnp.bfloat16)
    partial_value = jnp.dot(hidden, reduce_w, preferred_element_type=jnp.float32)
    mixed = lax.psum_scatter(
        partial_value.astype(jnp.bfloat16), "tensor", scatter_dimension=1, tiled=True
    ).astype(jnp.float32)
    updated = stream.reshape(positions, share).astype(jnp.float32) + scale * (mixed + bias_reduce)
    return updated.astype(jnp.bfloat16).reshape(height, width, share)


def per_device(
    features,
    depth_kernel,
    norm_gain,
    norm_bias,
    w_expand,
    b_expand,
    w_reduce,
    b_reduce,
    layer_scale,
):
    stream = features
    for block_id in range(BLOCKS):
        stream = one_block(
            stream,
            depth_kernel[block_id],
            norm_gain[block_id],
            norm_bias[block_id],
            w_expand[block_id],
            b_expand[block_id],
            w_reduce[block_id],
            b_reduce[block_id],
            layer_scale[block_id],
        )
    return stream


def solution(mesh):
    return jax.shard_map(
        per_device,
        mesh=mesh,
        in_specs=(
            P("space", None, "tensor"),
            P(None, None, None, "tensor"),
            P(),
            P(),
            P(None, None, "tensor"),
            P(None, "tensor"),
            P(None, "tensor", None),
            P(None, "tensor"),
            P(None, "tensor"),
        ),
        out_specs=P("space", None, "tensor"),
        check_vma=False,
    )
```

profile of v0, /device:TPU:8, one launch (start us, length us, event | category | flops | bytes accessed | tf_op | source)
XLA Modules:
  0.0 327.0 jit_solution(3460924509859641475)
XLA Ops:
  6.5 0.0 all-gather.3.cloned.1.call-start
  6.5 0.9 fusion.455
  7.4 6.1 %collective-permute-start = (bf16[3,128,64]{1,2,0:T(8,128)(2,1)S(1)}, bf16[3,128,64]{1,2,0:T(8,128)(2,1)S(1)}, u32[]{:S(2)}, u32[]{:S(2)}) collective-permute-start(bf16[3,128,64]{1,2,0:T(8,128)(2,1)S(1)} %get-tuple-element.17), channel_id=1, source_target_pairs={{0,16},{16,32},{32,48},{48,64},{64,80},{80,96},{96,112},{112,128},... | collective-permute-start | bytes 147464 | tf_op jit(solution)/shard_map/ppermute | solution.py:18
  13.5 6.7 %collective-permute-start.1 = (bf16[3,128,64]{1,2,0:T(8,128)(2,1)S(1)}, bf16[3,128,64]{1,2,0:T(8,128)(2,1)S(1)}, u32[]{:S(2)}, u32[]{:S(2)}) collective-permute-start(bf16[3,128,64]{1,2,0:T(8,128)(2,1)S(1)} %get-tuple-element.18), channel_id=1, source_target_pairs={{16,0},{32,16},{48,32},{64,48},{80,64},{96,80},{112,96},{128,112},... | collective-permute-start | bytes 147464 | tf_op jit(solution)/shard_map/ppermute | solution.py:19
  20.2 0.9 fusion.456
  21.1 0.8 fusion.457
  21.9 0.8 fusion.458
  22.7 0.1 fusion.288
  22.8 0.0 copy-start.1
  22.8 0.0 copy-start.4
  22.8 0.0 copy-start.5
  22.8 0.0 collective-permute-done
  22.8 0.5 collective-permute-done.1
  23.3 1.0 maximum_convert_fusion.1
  24.3 2.2 fusion.451
  26.5 29.5 %all-reduce.3 = (f32[512]{0:T(512)S(1)}, f32[512]{0:T(512)S(1)}) all-reduce(f32[512]{0:T(512)S(1)} %bitcast.584, f32[512]{0:T(512)S(1)} %bitcast.583), channel_id=1, replica_groups=mesh['space'=32,'tensor'=16] {'tensor'}, use_global_device_ids=true, to_apply=%region_3.4 | all-reduce | flops 1024 | bytes 8192 | tf_op jit(solution)/shard_map/psum | solution.py:40
  56.0 0.7 fusion.285
  56.7 0.0 all-gather.3.cloned.1.call-update
  56.7 0.0 reduce-scatter.3.cloned.1.call-start
  56.8 0.0 copy-done.1
  56.8 35.1 %all-gather.3.cloned.1.call-done = bf16[512,1024]{0,1:T(8,128)(2,1)} async-done(((bf16[512,64]{0,1:T(8,128)(2,1)}), bf16[512,1024]{0,1:T(8,128)(2,1)}) %all-gather.3.cloned.1.call-update) | async-done | bytes 1048592 | tf_op jit(solution)/shard_map/all_gather | solution.py:49
  91.8 0.0 copy-done.4
  91.8 0.0 copy-done.5
  91.8 4.6 %convolution_convert_fusion.1 = bf16[512,1024]{0,1:T(8,128)(2,1)} fusion(bf16[2,256,1024]{2,1,0:T(8,128)(2,1)S(1)} %copy-done.4, bf16[512,1024]{0,1:T(8,128)(2,1)} %all-gather.3.cloned.1.call-done, bf16[2,1024,256]{2,1,0:T(8,128)(2,1)S(1)} %copy-done.5, f32[256]{0:T(256)S(1)} %bitcast.588), kind=kOutput, calls=%fused_computation.85 | convolution fusion | flops 546045952 | bytes 3146752 | tf_op jit(solution)/shard_map/dot_general | solution.py:54
  96.4 0.0 copy-start.2
  96.4 0.0 reduce-scatter.3.cloned.1.call-update
  96.5 0.0 all-gather.5.cloned.1.call-start
  96.5 0.6 copy-done.2
  97.1 0.0 copy-done.3
  97.2 66.4 %reduce-scatter.3.cloned.1.call-done = bf16[512,64]{0,1:T(8,128)(2,1)} async-done(((bf16[512,1024]{0,1:T(8,128)(2,1)}), bf16[512,64]{0,1:T(8,128)(2,1)}) %reduce-scatter.3.cloned.1.call-update) | async-done | bytes 65552 | tf_op jit(solution)/shard_map/reduce_scatter | solution.py:55
  163.6 0.0 copy-done
  163.6 0.9 fusion.284
  164.6 5.5 %collective-permute-start.3 = (bf16[3,128,64]{1,0,2:T(4,128)(2,1)S(1)}, bf16[3,128,64]{1,0,2:T(4,128)(2,1)S(1)}, u32[]{:S(2)}, u32[]{:S(2)}) collective-permute-start(bf16[3,128,64]{1,0,2:T(4,128)(2,1)S(1)} %slice.780), channel_id=1, source_target_pairs={{16,0},{32,16},{48,32},{64,48},{80,64},{96,80},{112,96},{128,112},... | collective-permute-start | bytes 147464 | tf_op jit(solution)/shard_map/ppermute | solution.py:19
  170.1 1.9 collective-permute-start.2
  172.0 0.1 fusion.290
  172.1 0.0 collective-permute-done.3
  172.2 7.1 %collective-permute-done.2 = bf16[3,128,64]{1,0,2:T(4,128)(2,1)S(1)} collective-permute-done((bf16[3,128,64]{1,0,2:T(4,128)(2,1)S(1)}, bf16[3,128,64]{1,0,2:T(4,128)(2,1)S(1)}, u32[]{:S(2)}, u32[]{:S(2)}) %collective-permute-start.2) | collective-permute-done | bytes 49184 | tf_op jit(solution)/shard_map/ppermute | solution.py:18
  179.3 0.1 maximum_convert_fusion
  179.4 7.0 %fusion.450 = (f32[4,128]{1,0:T(4,128)S(1)}, f32[4,128]{1,0:T(4,128)S(1)}, f32[4,128,64]{1,0,2:T(4,128)S(1)}) fusion(f32[64]{0:T(128)S(1)} %get-tuple-element.22, f32[64]{0:T(128)S(1)} %get-tuple-element.23, f32[64]{0:T(128)S(1)} %get-tuple-element.24, f32[64]{0:T(128)S(1)} %get-tuple-element.25, f32[10,128,64]{1,0,2:T(8,128)S(1)} %maximum_convert_fusion, ...), kind=kLoop, calls=%fused_computation.684 | loop fusion | flops 3275776 | bytes 1602048 | tf_op jit(solution)/shard_map/reduce_sum | solution.py:41
  186.5 27.1 %all-reduce.2 = (f32[512]{0:T(512)S(1)}, f32[512]{0:T(512)S(1)}) all-reduce(f32[512]{0:T(512)S(1)} %bitcast.586, f32[512]{0:T(512)S(1)} %bitcast.585), channel_id=1, replica_groups=mesh['space'=32,'tensor'=16] {'tensor'}, use_global_device_ids=true, to_apply=%region_8.9 | all-reduce | flops 1024 | bytes 8192 | tf_op jit(solution)/shard_map/psum | solution.py:40
  213.6 0.7 fusion.286
  214.3 0.0 all-gather.5.cloned.1.call-update
  214.4 0.0 reduce-scatter.5.cloned.1.call-start
  214.4 32.7 %all-gather.5.cloned.1.call-done = bf16[512,1024]{0,1:T(8,128)(2,1)} async-done(((bf16[512,64]{0,1:T(8,128)(2,1)}), bf16[512,1024]{0,1:T(8,128)(2,1)}) %all-gather.5.cloned.1.call-update) | async-done | bytes 1048592 | tf_op jit(solution)/shard_map/all_gather | solution.py:49
  247.1 4.6 %convolution_convert_fusion = bf16[512,1024]{0,1:T(8,128)(2,1)} fusion(bf16[2,256,1024]{2,1,0:T(8,128)(2,1)S(1)} %copy-done.4, bf16[512,1024]{0,1:T(8,128)(2,1)} %all-gather.5.cloned.1.call-done, bf16[2,1024,256]{2,1,0:T(8,128)(2,1)S(1)} %copy-done.5, f32[256]{0:T(256)S(1)} %bitcast.587), kind=kOutput, calls=%fused_computation.84 | convolution fusion | flops 546045952 | bytes 3146752 | tf_op jit(solution)/shard_map/dot_general | solution.py:54
  251.7 0.0 reduce-scatter.5.cloned.1.call-update
  251.8 67.2 %reduce-scatter.5.cloned.1.call-done = bf16[512,64]{0,1:T(8,128)(2,1)} async-done(((bf16[512,1024]{0,1:T(8,128)(2,1)}), bf16[512,64]{0,1:T(8,128)(2,1)}) %reduce-scatter.5.cloned.1.call-update) | async-done | bytes 65552 | tf_op jit(solution)/shard_map/reduce_scatter | solution.py:55
  318.9 1.6 copy_bitcast_fusion
  (17 shorter events, 0.2 us)
Async XLA Ops:
  6.5 85.3 %all-gather.3.cloned.1.call-start = ((), (), s32[]{:S(2)}) async-start(), calls=%async_computation.2 | async-start | bytes 1114112 | tf_op jit(solution)/shard_map/all_gather | solution.py:49
  7.4 15.4 %collective-permute-start = (bf16[3,128,64]{1,2,0:T(8,128)(2,1)S(1)}, bf16[3,128,64]{1,2,0:T(8,128)(2,1)S(1)}, u32[]{:S(2)}, u32[]{:S(2)}) collective-permute-start(bf16[3,128,64]{1,2,0:T(8,128)(2,1)S(1)} %get-tuple-element.17), channel_id=1, source_target_pairs={{0,16},{16,32},{32,48},{48,64},{64,80},{80,96},{96,112},{112,128},... | collective-permute-start | bytes 147464 | tf_op jit(solution)/shard_map/ppermute | solution.py:18
  13.5 9.8 %collective-permute-start.1 = (bf16[3,128,64]{1,2,0:T(8,128)(2,1)S(1)}, bf16[3,128,64]{1,2,0:T(8,128)(2,1)S(1)}, u32[]{:S(2)}, u32[]{:S(2)}) collective-permute-start(bf16[3,128,64]{1,2,0:T(8,128)(2,1)S(1)} %get-tuple-element.18), channel_id=1, source_target_pairs={{16,0},{32,16},{48,32},{64,48},{80,64},{96,80},{112,96},{128,112},... | collective-permute-start | bytes 147464 | tf_op jit(solution)/shard_map/ppermute | solution.py:19
  22.8 34.0 %copy-start.1 = (f32[2,256]{1,0:T(2,128)S(1)}, f32[2,256]{1,0:T(2,128)}, u32[]{:S(2)}) copy-start(f32[2,256]{1,0:T(2,128)} %param.14) | copy-start | bytes 6148
  22.8 69.1 %copy-start.4 = (bf16[2,256,1024]{2,1,0:T(8,128)(2,1)S(1)}, bf16[2,256,1024]{2,1,0:T(8,128)(2,1)}, u32[]{:S(2)}) copy-start(bf16[2,256,1024]{2,1,0:T(8,128)(2,1)} %param.15) | copy-start | bytes 3145732
  22.8 69.1 %copy-start.5 = (bf16[2,1024,256]{2,1,0:T(8,128)(2,1)S(1)}, bf16[2,1024,256]{2,1,0:T(8,128)(2,1)}, u32[]{:S(2)}) copy-start(bf16[2,1024,256]{2,1,0:T(8,128)(2,1)} %param.13) | copy-start | bytes 3145732
  56.7 106.9 %reduce-scatter.3.cloned.1.call-start = ((), (), s32[]{:S(2)}) async-start(), calls=%async_computation.3 | async-start | bytes 1114112 | tf_op jit(solution)/shard_map/reduce_scatter | solution.py:55
  96.4 0.7 copy-start.2
  96.4 0.7 copy-start.3
  96.4 67.2 %copy-start = (bf16[4,128,64]{1,2,0:T(8,128)(2,1)S(1)}, bf16[4,128,64]{1,2,0:T(8,128)(2,1)}, u32[]{:S(2)}) copy-start(bf16[4,128,64]{1,2,0:T(8,128)(2,1)} %param.9) | copy-start | bytes 196612
  96.5 150.7 %all-gather.5.cloned.1.call-start = ((), (), s32[]{:S(2)}) async-start(), calls=%async_computation.4 | async-start | bytes 1114112 | tf_op jit(solution)/shard_map/all_gather | solution.py:49
  164.6 7.5 %collective-permute-start.3 = (bf16[3,128,64]{1,0,2:T(4,128)(2,1)S(1)}, bf16[3,128,64]{1,0,2:T(4,128)(2,1)S(1)}, u32[]{:S(2)}, u32[]{:S(2)}) collective-permute-start(bf16[3,128,64]{1,0,2:T(4,128)(2,1)S(1)} %slice.780), channel_id=1, source_target_pairs={{16,0},{32,16},{48,32},{64,48},{80,64},{96,80},{112,96},{128,112},... | collective-permute-start | bytes 147464 | tf_op jit(solution)/shard_map/ppermute | solution.py:19
  170.1 9.2 %collective-permute-start.2 = (bf16[3,128,64]{1,0,2:T(4,128)(2,1)S(1)}, bf16[3,128,64]{1,0,2:T(4,128)(2,1)S(1)}, u32[]{:S(2)}, u32[]{:S(2)}) collective-permute-start(bf16[3,128,64]{1,0,2:T(4,128)(2,1)S(1)} %slice.778), channel_id=1, source_target_pairs={{0,16},{16,32},{32,48},{48,64},{64,80},{80,96},{96,112},{112,128},... | collective-permute-start | bytes 147464 | tf_op jit(solution)/shard_map/ppermute | solution.py:18
  214.4 104.6 %reduce-scatter.5.cloned.1.call-start = ((), (), s32[]{:S(2)}) async-start(), calls=%async_computation.5 | async-start | bytes 1114112 | tf_op jit(solution)/shard_map/reduce_scatter | solution.py:55
Sparse Core Ops, SparseCore 0:
  56.8 34.9 all-gather.2
  96.6 66.9 reduce-scatter.2
  214.5 32.6 all-gather.4
  251.9 67.0 reduce-scatter.4
where the time goes:
time: 328 us; the launch traced here: 327 us
  waiting for transfers between devices  209 us (64%)
  blocking collectives  56.6 us (17%)
  starting transfers between devices  20.3 us (6%)
  other arithmetic  14.3 us (4%)
  between operations  13.3 us (4%)
  matrix products  9.2 us (3%)
  local copies, waits for them, and re-layouts  4.19 us (1%)
    reduce_scatter x2, waiting for transfers between devices, one_block(): lax.psum_scatter(partial_value.astype(jnp.bfloat16), 'tensor', scatter_di...  134 us
    all_gather x2, waiting for transfers between devices, one_block(): lax.all_gather(normed_part, 'tensor', axis=1, tiled=True)  67.8 us
    psum x2, blocking collectives, one_block(): lax.psum((jnp.sum(filtered, axis=-1), jnp.sum(filtered * filtered, axis=-...  56.6 us
    ppermute x2, starting transfers between devices, with_halo(): after = lax.ppermute(leading, axis, down)  12.1 us
    dot_general x2, matrix products, one_block(): jnp.dot(hidden, reduce_w, preferred_element_type=jnp.float32)  9.2 us
    reduce_sum x2, other arithmetic, one_block(): jnp.sum(filtered, axis=-1)  9.17 us
    ppermute x2, starting transfers between devices, with_halo(): before = lax.ppermute(last, axis, up)  8 us
    ppermute x2, waiting for transfers between devices, with_halo(): before = lax.ppermute(last, axis, up)  7.13 us
  transfers between devices with their start and end apart: 8, of which 6 were waited for; matrix products, arithmetic and copies ran while one was open for 1% of the time, Pallas kernels for 0%

commit v1 on v0

--- a/solution.py
+++ b/solution.py
@@ -46,7 +46,10 @@
         jnp.bfloat16
     )
     preact = jnp.dot(
-        lax.all_gather(normed_part, "tensor", axis=1, tiled=True),
+        jnp.concatenate(
+            lax.all_to_all(jnp.stack([normed_part] * lax.axis_size("tensor")), "tensor", 0, 0),
+            axis=1,
+        ),
         expand,
         preferred_element_type=jnp.float32,
     )

time: 328 us -> 290 us (0.88)
  waiting for transfers between devices: 209 us -> 150 us
  blocking collectives: 56.6 us -> 75.8 us
  starting transfers between devices: 20.3 us -> 24.2 us
    all_gather x2 -> x0, waiting for transfers between devices: 67.8 us -> none  [one_block(): lax.all_gather(normed_part, 'tensor', axis=1, tiled=True)]
    all_to_all x0 -> x1, blocking collectives: none -> 19.1 us  [one_block(): lax.all_to_all(jnp.stack([normed_part] * lax.axis_size('tensor')), 'tenso...]
    all_to_all x0 -> x1, waiting for transfers between devices: none -> 16.5 us  [one_block(): lax.all_to_all(jnp.stack([normed_part] * lax.axis_size('tensor')), 'tenso...]
    reduce_scatter x2, waiting for transfers between devices: 134 us -> 126 us  [one_block(): lax.psum_scatter(partial_value.astype(jnp.bfloat16), 'tensor', scatter_di...]
    all_to_all x0 -> x1, starting transfers between devices: none -> 3.78 us  [one_block(): lax.all_to_all(jnp.stack([normed_part] * lax.axis_size('tensor')), 'tenso...]
  transfers between devices with their start and end apart: 8 -> 7, of which waited for: 6 -> 5; matrix products, arithmetic and copies ran while one was open for 1% -> 1% of each run, Pallas kernels for 0% -> 0%
where the time goes in v1:
time: 290 us; the launch traced here: 289 us
  waiting for transfers between devices  150 us (52%)
  blocking collectives  75.8 us (26%)
  starting transfers between devices  24.2 us (8%)
  between operations  13.6 us (5%)
  other arithmetic  13 us (4%)
  matrix products  6.72 us (2%)
  local copies, waits for them, and re-layouts  5.36 us (2%)
    reduce_scatter x2, waiting for transfers between devices, one_block(): lax.psum_scatter(partial_value.astype(jnp.bfloat16), 'tensor', scatter_di...  126 us
    psum x2, blocking collectives, one_block(): lax.psum((jnp.sum(filtered, axis=-1), jnp.sum(filtered * filtered, axis=-...  56.7 us
    all_to_all x1, blocking collectives, one_block(): lax.all_to_all(jnp.stack([normed_part] * lax.axis_size('tensor')), 'tenso...  19.1 us
    all_to_all x1, waiting for transfers between devices, one_block(): lax.all_to_all(jnp.stack([normed_part] * lax.axis_size('tensor')), 'tenso...  16.5 us
    ppermute x2, starting transfers between devices, with_halo(): after = lax.ppermute(leading, axis, down)  12.3 us
    reduce_sum x2, other arithmetic, one_block(): jnp.sum(filtered, axis=-1)  9.19 us
    ppermute x2, starting transfers between devices, with_halo(): before = lax.ppermute(last, axis, up)  8 us
    ppermute x2, waiting for transfers between devices, with_halo(): before = lax.ppermute(last, axis, up)  7.19 us
  transfers between devices with their start and end apart: 7, of which 5 were waited for; matrix products, arithmetic and copies ran while one was open for 1% of the time, Pallas kernels for 0%

profile of v1, /device:TPU:8, one launch (start us, length us, event | category | flops | bytes accessed | tf_op | source)
XLA Modules:
  0.0 288.9 jit_solution(10442654575009390091)
XLA Ops:
  6.5 0.9 fusion.455
  7.4 6.1 %collective-permute-start = (bf16[3,128,64]{1,2,0:T(8,128)(2,1)S(1)}, bf16[3,128,64]{1,2,0:T(8,128)(2,1)S(1)}, u32[]{:S(2)}, u32[]{:S(2)}) collective-permute-start(bf16[3,128,64]{1,2,0:T(8,128)(2,1)S(1)} %get-tuple-element.17), channel_id=1, source_target_pairs={{0,16},{16,32},{32,48},{48,64},{64,80},{80,96},{96,112},{112,128},... | collective-permute-start | bytes 147464 | tf_op jit(solution)/shard_map/ppermute | solution.py:18
  13.5 6.7 %collective-permute-start.1 = (bf16[3,128,64]{1,2,0:T(8,128)(2,1)S(1)}, bf16[3,128,64]{1,2,0:T(8,128)(2,1)S(1)}, u32[]{:S(2)}, u32[]{:S(2)}) collective-permute-start(bf16[3,128,64]{1,2,0:T(8,128)(2,1)S(1)} %get-tuple-element.18), channel_id=1, source_target_pairs={{16,0},{32,16},{48,32},{64,48},{80,64},{96,80},{112,96},{128,112},... | collective-permute-start | bytes 147464 | tf_op jit(solution)/shard_map/ppermute | solution.py:19
  20.2 0.9 fusion.456
  21.1 0.8 fusion.457
  21.9 0.8 fusion.458
  22.7 0.1 fusion.288
  22.8 0.1 fusion.289
  22.8 0.0 collective-permute-done
  22.8 0.5 collective-permute-done.1
  23.3 0.9 maximum_convert_fusion.1
  24.2 2.2 fusion.451
  26.3 29.5 %all-reduce.3 = (f32[512]{0:T(512)S(1)}, f32[512]{0:T(512)S(1)}) all-reduce(f32[512]{0:T(512)S(1)} %bitcast.592, f32[512]{0:T(512)S(1)} %bitcast.591), channel_id=1, replica_groups=mesh['space'=32,'tensor'=16] {'tensor'}, use_global_device_ids=true, to_apply=%region_3.4 | all-reduce | flops 1024 | bytes 8192 | tf_op jit(solution)/shard_map/psum | solution.py:40
  55.9 0.1 fusion.285
  56.0 1.1 stack.4
  57.0 0.0 copy-start.1
  57.0 0.0 copy-start.4
  57.0 0.0 copy-start.5
  57.1 3.8 %all-to-all-start = ((bf16[16,512,64]{1,2,0:T(8,128)(2,1)}), bf16[16,512,64]{1,2,0:T(8,128)(2,1)S(1)}, u32[]{:S(2)}, u32[]{:S(2)}) async-start(bf16[16,512,64]{1,2,0:T(8,128)(2,1)} %stack.4), calls=%async_computation | async-start | bytes 2097152 | tf_op jit(solution)/shard_map/all_to_all | solution.py:50
  60.8 0.0 reduce-scatter.3.cloned.1.call-start
  60.9 0.0 copy-done.1
  60.9 16.5 %all-to-all-done = bf16[16,512,64]{1,2,0:T(8,128)(2,1)S(1)} async-done(((bf16[16,512,64]{1,2,0:T(8,128)(2,1)}), bf16[16,512,64]{1,2,0:T(8,128)(2,1)S(1)}, u32[]{:S(2)}, u32[]{:S(2)}) %all-to-all-start) | async-done | bytes 1048608 | tf_op jit(solution)/shard_map/all_to_all | solution.py:50
  77.4 0.0 copy-done.4
  77.4 0.0 copy-done.5
  77.4 3.4 %convolution_convert_fusion.1 = bf16[512,1024]{0,1:T(8,128)(2,1)} fusion(bf16[2,256,1024]{2,1,0:T(8,128)(2,1)S(1)} %copy-done.4, bf16[512,1024]{0,1:T(8,128)(2,1)S(1)} %bitcast.588, bf16[2,1024,256]{2,1,0:T(8,128)(2,1)S(1)} %copy-done.5, f32[256]{0:T(256)S(1)} %bitcast.596), kind=kOutput, calls=%fused_computation.85 | convolution fusion | flops 546045952 | bytes 3146752 | tf_op jit(solution)/shard_map/dot_general | solution.py:57
  80.8 0.0 copy-start.2
  80.8 0.0 copy-start.3
  80.8 0.0 reduce-scatter.3.cloned.1.call-update
  80.8 0.0 reduce-scatter.5.cloned.1.call-start
  80.9 0.6 copy-done.2
  81.5 0.0 copy-done.3
  81.5 63.9 %reduce-scatter.3.cloned.1.call-done = bf16[512,64]{0,1:T(8,128)(2,1)} async-done(((bf16[512,1024]{0,1:T(8,128)(2,1)}), bf16[512,64]{0,1:T(8,128)(2,1)}) %reduce-scatter.3.cloned.1.call-update) | async-done | bytes 65552 | tf_op jit(solution)/shard_map/reduce_scatter | solution.py:58
  145.4 0.0 copy-done
  145.4 0.9 fusion.284
  146.4 5.6 %collective-permute-start.3 = (bf16[3,128,64]{1,0,2:T(4,128)(2,1)S(1)}, bf16[3,128,64]{1,0,2:T(4,128)(2,1)S(1)}, u32[]{:S(2)}, u32[]{:S(2)}) collective-permute-start(bf16[3,128,64]{1,0,2:T(4,128)(2,1)S(1)} %slice.780), channel_id=1, source_target_pairs={{16,0},{32,16},{48,32},{64,48},{80,64},{96,80},{112,96},{128,112},... | collective-permute-start | bytes 147464 | tf_op jit(solution)/shard_map/ppermute | solution.py:19
  152.1 1.9 collective-permute-start.2
  154.1 0.0 collective-permute-done.3
  154.1 7.2 %collective-permute-done.2 = bf16[3,128,64]{1,0,2:T(4,128)(2,1)S(1)} collective-permute-done((bf16[3,128,64]{1,0,2:T(4,128)(2,1)S(1)}, bf16[3,128,64]{1,0,2:T(4,128)(2,1)S(1)}, u32[]{:S(2)}, u32[]{:S(2)}) %collective-permute-start.2) | collective-permute-done | bytes 49184 | tf_op jit(solution)/shard_map/ppermute | solution.py:18
  161.3 0.1 maximum_convert_fusion
  161.4 7.0 %fusion.450 = (f32[4,128]{1,0:T(4,128)S(1)}, f32[4,128]{1,0:T(4,128)S(1)}, f32[4,128,64]{1,0,2:T(4,128)S(1)}) fusion(f32[64]{0:T(128)S(1)} %get-tuple-element.22, f32[64]{0:T(128)S(1)} %get-tuple-element.23, f32[64]{0:T(128)S(1)} %get-tuple-element.24, f32[64]{0:T(128)S(1)} %get-tuple-element.25, f32[10,128,64]{1,0,2:T(8,128)S(1)} %maximum_convert_fusion, ...), kind=kLoop, calls=%fused_computation.684 | loop fusion | flops 3275776 | bytes 1602048 | tf_op jit(solution)/shard_map/reduce_sum | solution.py:41
  168.4 27.1 %all-reduce.2 = (f32[512]{0:T(512)S(1)}, f32[512]{0:T(512)S(1)}) all-reduce(f32[512]{0:T(512)S(1)} %bitcast.594, f32[512]{0:T(512)S(1)} %bitcast.593), channel_id=1, replica_groups=mesh['space'=32,'tensor'=16] {'tensor'}, use_global_device_ids=true, to_apply=%region_8.9 | all-reduce | flops 1024 | bytes 8192 | tf_op jit(solution)/shard_map/psum | solution.py:40
  195.6 0.1 fusion.286
  195.7 0.1 stack.5
  195.8 19.1 %all_to_all.10 = bf16[16,512,64]{1,2,0:T(8,128)(2,1)S(1)} all-to-all(bf16[16,512,64]{1,2,0:T(8,128)(2,1)S(1)} %stack.5), channel_id=1, replica_groups=mesh['space'=32,'tensor'=16] {'tensor'}, dimensions={0} | all-to-all | bytes 2097152 | tf_op jit(solution)/shard_map/all_to_all | solution.py:50
  214.9 3.4 %convolution_convert_fusion = bf16[512,1024]{0,1:T(8,128)(2,1)} fusion(bf16[2,256,1024]{2,1,0:T(8,128)(2,1)S(1)} %copy-done.4, bf16[512,1024]{0,1:T(8,128)(2,1)S(1)} %bitcast.589, bf16[2,1024,256]{2,1,0:T(8,128)(2,1)S(1)} %copy-done.5, f32[256]{0:T(256)S(1)} %bitcast.595), kind=kOutput, calls=%fused_computation.84 | convolution fusion | flops 546045952 | bytes 3146752 | tf_op jit(solution)/shard_map/dot_general | solution.py:57
  218.3 0.0 reduce-scatter.5.cloned.1.call-update
  218.3 62.2 %reduce-scatter.5.cloned.1.call-done = bf16[512,64]{0,1:T(8,128)(2,1)} async-done(((bf16[512,1024]{0,1:T(8,128)(2,1)}), bf16[512,64]{0,1:T(8,128)(2,1)}) %reduce-scatter.5.cloned.1.call-update) | async-done | bytes 65552 | tf_op jit(solution)/shard_map/reduce_scatter | solution.py:58
  280.5 1.6 copy_bitcast_fusion
  (16 shorter events, 0.2 us)
Async XLA Ops:
  7.4 15.4 %collective-permute-start = (bf16[3,128,64]{1,2,0:T(8,128)(2,1)S(1)}, bf16[3,128,64]{1,2,0:T(8,128)(2,1)S(1)}, u32[]{:S(2)}, u32[]{:S(2)}) collective-permute-start(bf16[3,128,64]{1,2,0:T(8,128)(2,1)S(1)} %get-tuple-element.17), channel_id=1, source_target_pairs={{0,16},{16,32},{32,48},{48,64},{64,80},{80,96},{96,112},{112,128},... | collective-permute-start | bytes 147464 | tf_op jit(solution)/shard_map/ppermute | solution.py:18
  13.5 9.8 %collective-permute-start.1 = (bf16[3,128,64]{1,2,0:T(8,128)(2,1)S(1)}, bf16[3,128,64]{1,2,0:T(8,128)(2,1)S(1)}, u32[]{:S(2)}, u32[]{:S(2)}) collective-permute-start(bf16[3,128,64]{1,2,0:T(8,128)(2,1)S(1)} %get-tuple-element.18), channel_id=1, source_target_pairs={{16,0},{32,16},{48,32},{64,48},{80,64},{96,80},{112,96},{128,112},... | collective-permute-start | bytes 147464 | tf_op jit(solution)/shard_map/ppermute | solution.py:19
  57.0 3.8 %copy-start.1 = (f32[2,256]{1,0:T(2,128)S(1)}, f32[2,256]{1,0:T(2,128)}, u32[]{:S(2)}) copy-start(f32[2,256]{1,0:T(2,128)} %param.14) | copy-start | bytes 6148
  57.0 20.4 %copy-start.4 = (bf16[2,256,1024]{2,1,0:T(8,128)(2,1)S(1)}, bf16[2,256,1024]{2,1,0:T(8,128)(2,1)}, u32[]{:S(2)}) copy-start(bf16[2,256,1024]{2,1,0:T(8,128)(2,1)} %param.15) | copy-start | bytes 3145732
  57.0 20.4 %copy-start.5 = (bf16[2,1024,256]{2,1,0:T(8,128)(2,1)S(1)}, bf16[2,1024,256]{2,1,0:T(8,128)(2,1)}, u32[]{:S(2)}) copy-start(bf16[2,1024,256]{2,1,0:T(8,128)(2,1)} %param.13) | copy-start | bytes 3145732
  57.1 20.4 %all-to-all-start = ((bf16[16,512,64]{1,2,0:T(8,128)(2,1)}), bf16[16,512,64]{1,2,0:T(8,128)(2,1)S(1)}, u32[]{:S(2)}, u32[]{:S(2)}) async-start(bf16[16,512,64]{1,2,0:T(8,128)(2,1)} %stack.4), calls=%async_computation | async-start | bytes 2097152 | tf_op jit(solution)/shard_map/all_to_all | solution.py:50
  60.8 84.6 %reduce-scatter.3.cloned.1.call-start = ((), (), s32[]{:S(2)}) async-start(), calls=%async_computation.4 | async-start | bytes 1114112 | tf_op jit(solution)/shard_map/reduce_scatter | solution.py:58
  80.8 0.7 copy-start.2
  80.8 0.7 copy-start.3
  80.8 64.6 %copy-start = (bf16[4,128,64]{1,2,0:T(8,128)(2,1)S(1)}, bf16[4,128,64]{1,2,0:T(8,128)(2,1)}, u32[]{:S(2)}) copy-start(bf16[4,128,64]{1,2,0:T(8,128)(2,1)} %param.9) | copy-start | bytes 196612
  80.8 199.7 %reduce-scatter.5.cloned.1.call-start = ((), (), s32[]{:S(2)}) async-start(), calls=%async_computation.5 | async-start | bytes 1114112 | tf_op jit(solution)/shard_map/reduce_scatter | solution.py:58
  146.4 7.6 %collective-permute-start.3 = (bf16[3,128,64]{1,0,2:T(4,128)(2,1)S(1)}, bf16[3,128,64]{1,0,2:T(4,128)(2,1)S(1)}, u32[]{:S(2)}, u32[]{:S(2)}) collective-permute-start(bf16[3,128,64]{1,0,2:T(4,128)(2,1)S(1)} %slice.780), channel_id=1, source_target_pairs={{16,0},{32,16},{48,32},{64,48},{80,64},{96,80},{112,96},{128,112},... | collective-permute-start | bytes 147464 | tf_op jit(solution)/shard_map/ppermute | solution.py:19
  152.1 9.2 %collective-permute-start.2 = (bf16[3,128,64]{1,0,2:T(4,128)(2,1)S(1)}, bf16[3,128,64]{1,0,2:T(4,128)(2,1)S(1)}, u32[]{:S(2)}, u32[]{:S(2)}) collective-permute-start(bf16[3,128,64]{1,0,2:T(4,128)(2,1)S(1)} %slice.778), channel_id=1, source_target_pairs={{0,16},{16,32},{32,48},{48,64},{64,80},{80,96},{96,112},{112,128},... | collective-permute-start | bytes 147464 | tf_op jit(solution)/shard_map/ppermute | solution.py:18
Sparse Core Ops, SparseCore 0:
  80.9 64.4 reduce-scatter.2
  218.4 62.0 reduce-scatter.4
